TPU v7x, 32 devices: a whole 2x2x4 slice. The times are simulated.
32 devices in a mesh: seq: 16 (over z, y, x), tensor: 2 (over core).
Axes of the slice: x: 2, y: 2, z: 4, core: 2. Of those that a mesh axis runs over, the one named last changes fastest.
Arguments:
- tokens: bfloat16 [1024, 4096], P('seq', 'tensor'), may hold values from -6 to 6
- w_gate: bfloat16 [16, 4096, 4096], P('seq', None, 'tensor'), may hold values from -0.09375 to 0.09375
- w_up: bfloat16 [16, 4096, 4096], P('seq', None, 'tensor'), may hold values from -0.09375 to 0.09375
- w_down: bfloat16 [16, 4096, 4096], P('seq', None, 'tensor'), may hold values from -0.0625 to 0.0625
- routes: int32 [8, 2], replicated, may hold values from 0 to 7, all different within a row; in each aligned block of 8 rows (0 to 7, 8 to 15, ...) at most 3 rows name the same one
- gate_values: float32 [8, 2], replicated, may hold values from 0.1 to 0.9
Outputs:
- moe_out: bfloat16 [1024, 4096], P('seq', 'tensor')
Inputs may be any that keep to these rules, and one draw needn't show every extreme that they name: `routes`: the two experts of a block differ; every expert is named by some block and by at most 3 blocks, and one by exactly 3.
All inputs are finite; a program needn't handle non-finite values.
Results may differ from a plain program's by a relative error of at most 0.005.
Values may be sent and summed in bfloat16 or wider, within the bound.
No kernel may reach another device: no remote copies, remote signals or barrier semaphores. Data moves between devices by JAX's collectives and lax.ppermute only.
A program may use at most 128 MiB of HBM per device.

v0:
```python
import jax
import jax.numpy as jnp
from jax import lax
from jax.sharding import PartitionSpec as P

E = 8


def route_slots(routes, gate_values, expert, capacity):
    block_count = routes.shape[0]
    matches = routes == expert
    member = jnp.any(matches, axis=1).astype(jnp.int32)
    weight = jnp.sum(jnp.where(matches, gate_values, 0.0), axis=1)
    position = jnp.cumsum(member) - 1
    slot_ids = jnp.arange(capacity, dtype=jnp.int32)
    picked = (member[None, :] == 1) & (position[None, :] == slot_ids[:, None])
    block_ids = jnp.arange(block_count, dtype=jnp.int32)
    block_index = jnp.sum(jnp.where(picked, block_ids[None, :], 0), axis=1)
    slot_gate = jnp.sum(jnp.where(picked, weight[None, :], 0.0), axis=1)
    return (picked, block_index, slot_gate)


def per_device(tokens, w_gate, w_up, w_down, routes, gate_values):
    seq_count = lax.axis_size("seq")
    part_count = seq_count // E
    expert = lax.axis_index("seq") // part_count
    block_count = routes.shape[0]
    capacity = 3 * block_count // 8
    columns = lax.all_gather(tokens, "seq", axis=0, tiled=True)
    block_rows = columns.shape[0] // block_count
    feature_width = columns.shape[1]
    picked, block_index, slot_gate = route_slots(routes, gate_values, expert, capacity)
    chosen = columns.reshape(block_count, block_rows, feature_width)[block_index]
    chosen = chosen.reshape(capacity * block_rows, feature_width)
    gate_cols = w_gate[0]
    up_cols = w_up[0]
    full_rows = lax.all_gather(chosen, "tensor", axis=1, tiled=True)
    gate_sum = jnp.dot(full_rows, gate_cols, preferred_element_type=jnp.float32)
    up_sum = jnp.dot(full_rows, up_cols, preferred_element_type=jnp.float32)
    hidden = (jax.nn.silu(gate_sum) * up_sum).astype(jnp.bfloat16)
    quarter = lax.all_gather(hidden, "tensor", axis=1, tiled=True)
    partial_value = jnp.dot(quarter, w_down[0], preferred_element_type=jnp.float32)
    weighted = partial_value.reshape(capacity, block_rows, feature_width) * slot_gate[:, None, None]
    scattered = jnp.einsum(
        "lb,lrd->brd", picked.astype(jnp.float32), weighted, precision=lax.Precision.HIGHEST
    )
    scattered = scattered.reshape(block_count * block_rows, feature_width)
    summed = lax.psum_scatter(scattered, "seq", scatter_dimension=0, tiled=True)
    return summed.astype(jnp.bfloat16)


def solution(mesh):
    placed = (
        P("seq", "tensor"),
        P("seq", None, "tensor"),
        P("seq", None, "tensor"),
        P("seq", None, "tensor"),
        P(),
        P(),
    )
    return jax.shard_map(
        per_device, mesh=mesh, in_specs=placed, out_specs=P("seq", "tensor"), check_vma=False
    )
```

profile of v0, /device:TPU:10, one launch (start us, length us, event | category | flops | bytes accessed | tf_op | source)
XLA Modules:
  0.0 356.7 jit_solution(6207690128557403853)
XLA Ops:
  6.5 0.7 all-gather.4.cloned.1.call-update
  7.3 0.0 all-gather.6.cloned.1.call-start
  7.3 0.7 fusion.13
  8.0 0.2 reduce-window.8
  8.2 0.1 select_reduce_fusion.1
  8.4 78.5 %all-gather.4.cloned.1.call-done = bf16[1024,2048]{1,0:T(8,128)(2,1)} async-done(((bf16[64,2048]{1,0:T(8,128)(2,1)}), bf16[1024,2048]{1,0:T(8,128)(2,1)}) %all-gather.4.cloned.1.call-update) | async-done | bytes 4194320 | tf_op jit(solution)/shard_map/all_gather | solution.py:29
  86.8 4.1 %gather_fusion = bf16[3,128,2048]{2,1,0:T(8,128)(2,1)} fusion(bf16[8,128,2048]{2,1,0:T(8,128)(2,1)} %bitcast.32, s32[1024]{0:T(1024)S(1)} %pad_clamp_fusion), kind=kCustom, calls=%fused_computation | custom fusion | bytes 3145740 | tf_op jit(solution)/shard_map/gather | solution.py:33
  90.9 0.0 all-gather.6.cloned.1.call-update
  90.9 0.0 all-gather.8.cloned.1.call-start
  91.0 11.1 %all-gather.6.cloned.1.call-done = bf16[384,4096]{1,0:T(8,128)(2,1)} async-done(((bf16[384,2048]{1,0:T(8,128)(2,1)}), bf16[384,4096]{1,0:T(8,128)(2,1)}) %all-gather.6.cloned.1.call-update) | async-done | bytes 3145744 | tf_op jit(solution)/shard_map/all_gather | solution.py:37
  102.1 13.2 %fusion.4 = f32[384,2048]{1,0:T(8,128)S(1)} fusion(bf16[384,4096]{1,0:T(8,128)(2,1)} %all-gather.6.cloned.1.call-done, bf16[1,4096,2048]{2,1,0:T(8,128)(2,1)} %param.7), kind=kOutput, calls=%fused_computation.5 | convolution fusion | flops 6442450944 | bytes 23068672 | tf_op jit(solution)/shard_map/dot_general | solution.py:38
  115.3 0.0 copy-start
  115.3 0.0 copy-start.1
  115.3 11.3 %multiply_convert_fusion = bf16[384,2048]{1,0:T(8,128)(2,1)} fusion(f32[384,2048]{1,0:T(8,128)S(1)} %fusion.4, bf16[384,4096]{1,0:T(8,128)(2,1)S(1)} %copy-done.2, bf16[1,4096,2048]{2,1,0:T(8,128)(2,1)} %param.8), kind=kOutput, calls=%fused_computation.9 | convolution fusion | flops 6447169536 | bytes 24641536 | tf_op jit(solution)/shard_map/dot_general | solution.py:39
  126.7 0.0 all-gather.8.cloned.1.call-update
  126.7 0.0 reduce-scatter.2.cloned.1.call-start
  126.8 0.1 select_reduce_fusion
  126.9 13.2 %all-gather.8.cloned.1.call-done = bf16[384,4096]{1,0:T(8,128)(2,1)} async-done(((bf16[384,2048]{1,0:T(8,128)(2,1)}), bf16[384,4096]{1,0:T(8,128)(2,1)}) %all-gather.8.cloned.1.call-update) | async-done | bytes 3145744 | tf_op jit(solution)/shard_map/all_gather | solution.py:41
  140.2 11.3 %fusion = f32[3,128,2048]{2,1,0:T(8,128)S(1)} fusion(bf16[3,128,4096]{2,1,0:T(8,128)(2,1)} %bitcast.33, bf16[1,4096,2048]{2,1,0:T(8,128)(2,1)} %param.9), kind=kOutput, calls=%fused_computation.1 | convolution fusion | flops 6442450944 | bytes 23068672 | tf_op jit(solution)/shard_map/dot_general | solution.py:42
  151.5 6.7 %fusion.6 = f32[8,128,2048]{2,0,1:T(8,128)S(1)} fusion(f32[3,128,2048]{2,1,0:T(8,128)S(1)} %fusion, f32[3]{0:T(128)S(1)} %select_reduce_fusion, s32[8]{0:T(128)S(1)} %add_bitcast_fusion, pred[8]{0:T(512)(128)(4,1)S(1)} %get-tuple-element.5), kind=kOutput, calls=%fused_computation.8 | convolution fusion | flops 76283952 | bytes 11534388 | tf_op jit(solution)/shard_map/lb,lrd->brd/dot_general | solution.py:44
  158.2 8.1 %copy.7 = f32[8,128,2048]{2,1,0:T(8,128)} copy(f32[8,128,2048]{2,0,1:T(8,128)S(1)} %fusion.6) | data formatting | bytes 16777216 | tf_op jit(solution)/shard_map/lb,lrd->brd/dot_general | solution.py:44
  166.3 0.0 reduce-scatter.2.cloned.1.call-update
  166.3 182.1 %reduce-scatter.2.cloned.1.call-done = f32[64,2048]{1,0:T(8,128)} async-done(((f32[1024,2048]{1,0:T(8,128)}), f32[64,2048]{1,0:T(8,128)}) %reduce-scatter.2.cloned.1.call-update) | async-done | bytes 524304 | tf_op jit(solution)/shard_map/reduce_scatter | solution.py:48
  348.4 1.8 convert_element_type.32
  (10 shorter events, 0.1 us)
Async XLA Ops:
  6.5 80.3 %all-gather.4.cloned.1.call-start = ((), (), s32[]{:S(2)}) async-start(), calls=%async_computation.1 | async-start | bytes 4456448 | tf_op jit(solution)/shard_map/all_gather | solution.py:29
  7.3 94.8 %all-gather.6.cloned.1.call-start = ((), (), s32[]{:S(2)}) async-start(), calls=%async_computation.2 | async-start | bytes 4718592 | tf_op jit(solution)/shard_map/all_gather | solution.py:37
  90.9 49.2 %all-gather.8.cloned.1.call-start = ((), (), s32[]{:S(2)}) async-start(), calls=%async_computation.3 | async-start | bytes 4718592 | tf_op jit(solution)/shard_map/all_gather | solution.py:41
  102.1 13.2 %copy-start.2 = (bf16[384,4096]{1,0:T(8,128)(2,1)S(1)}, bf16[384,4096]{1,0:T(8,128)(2,1)}, u32[]{:S(2)}) copy-start(bf16[384,4096]{1,0:T(8,128)(2,1)} %all-gather.6.cloned.1.call-done) | copy-start | bytes 9437188
  115.3 11.5 %copy-start = (s32[8,2]{0,1:T(2,128)S(1)}, s32[8,2]{0,1:T(2,128)}, u32[]{:S(2)}) copy-start(s32[8,2]{0,1:T(2,128)} %param.10) | copy-start | bytes 196
  115.3 11.4 %copy-start.1 = (f32[8,2]{0,1:T(2,128)S(1)}, f32[8,2]{0,1:T(2,128)}, u32[]{:S(2)}) copy-start(f32[8,2]{0,1:T(2,128)} %param.11) | copy-start | bytes 196
  126.7 221.7 %reduce-scatter.2.cloned.1.call-start = ((), (), s32[]{:S(2)}) async-start(), calls=%async_computation.4 | async-start | bytes 8912896 | tf_op jit(solution)/shard_map/reduce_scatter | solution.py:48
Sparse Core Ops, SparseCore 0:
  10.1 76.6 all-gather.3
  91.0 10.9 all-gather.5
  126.8 13.2 all-gather.7
  166.4 181.9 reduce-scatter.1
where the time goes:
time: 357 us
  waiting for transfers between devices  286 us (80%)
  matrix products  42.6 us (12%)
  between operations  13.2 us (4%)
  local copies, waits for them, and re-layouts  12.2 us (3%)
    reduce_scatter x1, waiting for transfers between devices, per_device(): summed = lax.psum_scatter(scattered, 'seq', scatter_dimension=0, tiled=True)  182 us
    all_gather x1, waiting for transfers between devices, per_device(): columns = lax.all_gather(tokens, 'seq', axis=0, tiled=True)  78.5 us
    all_gather x1, waiting for transfers between devices, per_device(): quarter = lax.all_gather(hidden, 'tensor', axis=1, tiled=True)  13.2 us
    dot_general x1, matrix products, per_device(): gate_sum = jnp.dot(full_rows, gate_cols, preferred_element_type=jnp.float32)  13.2 us
    dot_general x1, matrix products, per_device(): up_sum = jnp.dot(full_rows, up_cols, preferred_element_type=jnp.float32)  11.3 us
    dot_general x1, matrix products, per_device(): jnp.dot(quarter, w_down[0], preferred_element_type=jnp.float32)  11.3 us
    all_gather x1, waiting for transfers between devices, per_device(): full_rows = lax.all_gather(chosen, 'tensor', axis=1, tiled=True)  11.1 us
    dot_general x1, local copies, waits for them, and re-layouts, per_device(): jnp.einsum('lb,lrd->brd', picked.astype(jnp.float32), weighted, precision...  8.08 us
  transfers between devices with their start and end apart: 4, of which 4 were waited for; matrix products, arithmetic and copies ran while one was open for 0% of the time, Pallas kernels for 0%

commit v1 on v0

--- a/solution.py
+++ b/solution.py
@@ -26,7 +26,8 @@
     expert = lax.axis_index("seq") // part_count
     block_count = routes.shape[0]
     capacity = 3 * block_count // 8
-    columns = lax.all_gather(tokens, "seq", axis=0, tiled=True)
+    n_now = jax.lax.all_to_all(jnp.stack(jax.lax.axis_size("seq") * [tokens]), "seq", 0, 0)
+    columns = jnp.concatenate(n_now, 0)
     block_rows = columns.shape[0] // block_count
     feature_width = columns.shape[1]
     picked, block_index, slot_gate = route_slots(routes, gate_values, expert, capacity)

time: 357 us -> 383 us (1.073)
  waiting for transfers between devices: 286 us -> 301 us
  starting transfers between devices: 0.12 us -> 7.45 us
    all_to_all x0 -> x1, waiting for transfers between devices: none -> 91.4 us  [per_device(): jax.lax.all_to_all(jnp.stack(jax.lax.axis_size('seq') * [tokens]), 'seq',...]
    all_gather x1 -> x0, waiting for transfers between devices: 78.5 us -> none  [per_device(): columns = lax.all_gather(tokens, 'seq', axis=0, tiled=True)]
    all_to_all x0 -> x1, starting transfers between devices: none -> 7.33 us  [per_device(): jax.lax.all_to_all(jnp.stack(jax.lax.axis_size('seq') * [tokens]), 'seq',...]
where the time goes in v1:
time: 383 us; the launch traced here: 382 us
  waiting for transfers between devices  301 us (79%)
  matrix products  42.6 us (11%)
  local copies, waits for them, and re-layouts  15.6 us (4%)
  between operations  13.2 us (3%)
  starting transfers between devices  7.45 us (2%)
    reduce_scatter x1, waiting for transfers between devices, per_device(): summed = lax.psum_scatter(scattered, 'seq', scatter_dimension=0, tiled=True)  182 us
    all_to_all x1, waiting for transfers between devices, per_device(): jax.lax.all_to_all(jnp.stack(jax.lax.axis_size('seq') * [tokens]), 'seq',...  91.4 us
    all_gather x1, waiting for transfers between devices, per_device(): full_rows = lax.all_gather(chosen, 'tensor', axis=1, tiled=True)  14.5 us
    all_gather x1, waiting for transfers between devices, per_device(): quarter = lax.all_gather(hidden, 'tensor', axis=1, tiled=True)  13.2 us
    dot_general x1, matrix products, per_device(): gate_sum = jnp.dot(full_rows, gate_cols, preferred_element_type=jnp.float32)  13.2 us
    dot_general x1, matrix products, per_device(): up_sum = jnp.dot(full_rows, up_cols, preferred_element_type=jnp.float32)  11.4 us
    dot_general x1, matrix products, per_device(): jnp.dot(quarter, w_down[0], preferred_element_type=jnp.float32)  11.3 us
    dot_general x1, local copies, waits for them, and re-layouts, per_device(): jnp.einsum('lb,lrd->brd', picked.astype(jnp.float32), weighted, precision...  8.08 us
  transfers between devices with their start and end apart: 4, of which 4 were waited for; matrix products, arithmetic and copies ran while one was open for 0% of the time, Pallas kernels for 0%

profile of v1, /device:TPU:10, one launch (start us, length us, event | category | flops | bytes accessed | tf_op | source)
XLA Modules:
  0.0 382.4 jit_solution(5776492369834108686)
XLA Ops:
  6.5 3.4 stack.2
  10.0 7.3 %all-to-all-start = ((bf16[16,64,2048]{2,1,0:T(8,128)(2,1)}), bf16[16,64,2048]{2,1,0:T(8,128)(2,1)}, u32[]{:S(2)}, u32[]{:S(2)}) async-start(bf16[16,64,2048]{2,1,0:T(8,128)(2,1)} %stack.2), calls=%async_computation | async-start | bytes 8388608 | tf_op jit(solution)/shard_map/all_to_all | solution.py:29
  17.3 0.0 all-gather.3.cloned.1.call-start
  17.4 0.0 copy-done
  17.4 0.2 reduce-window.8
  17.6 0.1 select_reduce_fusion.1
  17.7 91.4 %all-to-all-done = bf16[16,64,2048]{2,1,0:T(8,128)(2,1)} async-done(((bf16[16,64,2048]{2,1,0:T(8,128)(2,1)}), bf16[16,64,2048]{2,1,0:T(8,128)(2,1)}, u32[]{:S(2)}, u32[]{:S(2)}) %all-to-all-start) | async-done | bytes 4194336 | tf_op jit(solution)/shard_map/all_to_all | solution.py:29
  109.1 4.1 %gather_fusion = bf16[3,128,2048]{2,1,0:T(8,128)(2,1)} fusion(bf16[8,128,2048]{2,1,0:T(8,128)(2,1)} %bitcast.3, s32[1024]{0:T(1024)S(1)} %pad_clamp_fusion), kind=kCustom, calls=%fused_computation | custom fusion | bytes 3145740 | tf_op jit(solution)/shard_map/gather | solution.py:34
  113.1 0.0 all-gather.3.cloned.1.call-update
  113.2 0.0 all-gather.5.cloned.1.call-start
  113.2 14.5 %all-gather.3.cloned.1.call-done = bf16[384,4096]{1,0:T(8,128)(2,1)} async-done(((bf16[384,2048]{1,0:T(8,128)(2,1)}), bf16[384,4096]{1,0:T(8,128)(2,1)}) %all-gather.3.cloned.1.call-update) | async-done | bytes 3145744 | tf_op jit(solution)/shard_map/all_gather | solution.py:38
  127.8 13.2 %fusion.4 = f32[384,2048]{1,0:T(8,128)S(1)} fusion(bf16[384,4096]{1,0:T(8,128)(2,1)} %all-gather.3.cloned.1.call-done, bf16[1,4096,2048]{2,1,0:T(8,128)(2,1)} %param.7), kind=kOutput, calls=%fused_computation.5 | convolution fusion | flops 6442450944 | bytes 23068672 | tf_op jit(solution)/shard_map/dot_general | solution.py:39
  141.0 0.0 copy-start.1
  141.0 11.4 %multiply_convert_fusion = bf16[384,2048]{1,0:T(8,128)(2,1)} fusion(f32[384,2048]{1,0:T(8,128)S(1)} %fusion.4, bf16[384,4096]{1,0:T(8,128)(2,1)S(1)} %copy-done.2, bf16[1,4096,2048]{2,1,0:T(8,128)(2,1)} %param.8), kind=kOutput, calls=%fused_computation.9 | convolution fusion | flops 6447169536 | bytes 24641536 | tf_op jit(solution)/shard_map/dot_general | solution.py:40
  152.4 0.0 all-gather.5.cloned.1.call-update
  152.4 0.0 reduce-scatter.2.cloned.1.call-start
  152.5 0.1 select_reduce_fusion
  152.6 13.2 %all-gather.5.cloned.1.call-done = bf16[384,4096]{1,0:T(8,128)(2,1)} async-done(((bf16[384,2048]{1,0:T(8,128)(2,1)}), bf16[384,4096]{1,0:T(8,128)(2,1)}) %all-gather.5.cloned.1.call-update) | async-done | bytes 3145744 | tf_op jit(solution)/shard_map/all_gather | solution.py:42
  165.8 11.3 %fusion = f32[3,128,2048]{2,1,0:T(8,128)S(1)} fusion(bf16[3,128,4096]{2,1,0:T(8,128)(2,1)} %bitcast.32, bf16[1,4096,2048]{2,1,0:T(8,128)(2,1)} %param.9), kind=kOutput, calls=%fused_computation.1 | convolution fusion | flops 6442450944 | bytes 23068672 | tf_op jit(solution)/shard_map/dot_general | solution.py:43
  177.2 6.7 %fusion.6 = f32[8,128,2048]{2,0,1:T(8,128)S(1)} fusion(f32[3,128,2048]{2,1,0:T(8,128)S(1)} %fusion, f32[3]{0:T(128)S(1)} %select_reduce_fusion, s32[8]{0:T(128)S(1)} %add_bitcast_fusion, pred[8]{0:T(512)(128)(4,1)S(1)} %get-tuple-element.5), kind=kOutput, calls=%fused_computation.8 | convolution fusion | flops 76283952 | bytes 11534388 | tf_op jit(solution)/shard_map/lb,lrd->brd/dot_general | solution.py:45
  183.9 8.1 %copy.7 = f32[8,128,2048]{2,1,0:T(8,128)} copy(f32[8,128,2048]{2,0,1:T(8,128)S(1)} %fusion.6) | data formatting | bytes 16777216 | tf_op jit(solution)/shard_map/lb,lrd->brd/dot_general | solution.py:45
  192.0 0.0 reduce-scatter.2.cloned.1.call-update
  192.0 182.1 %reduce-scatter.2.cloned.1.call-done = f32[64,2048]{1,0:T(8,128)} async-done(((f32[1024,2048]{1,0:T(8,128)}), f32[64,2048]{1,0:T(8,128)}) %reduce-scatter.2.cloned.1.call-update) | async-done | bytes 524304 | tf_op jit(solution)/shard_map/reduce_scatter | solution.py:49
  374.1 1.8 convert_element_type.32
  (10 shorter events, 0.1 us)
Async XLA Ops:
  10.0 7.4 %copy-start = (s32[8,2]{0,1:T(2,128)S(1)}, s32[8,2]{0,1:T(2,128)}, u32[]{:S(2)}) copy-start(s32[8,2]{0,1:T(2,128)} %param.10) | copy-start | bytes 196
  10.0 99.1 %all-to-all-start = ((bf16[16,64,2048]{2,1,0:T(8,128)(2,1)}), bf16[16,64,2048]{2,1,0:T(8,128)(2,1)}, u32[]{:S(2)}, u32[]{:S(2)}) async-start(bf16[16,64,2048]{2,1,0:T(8,128)(2,1)} %stack.2), calls=%async_computation | async-start | bytes 8388608 | tf_op jit(solution)/shard_map/all_to_all | solution.py:29
  17.3 110.5 %all-gather.3.cloned.1.call-start = ((), (), s32[]{:S(2)}) async-start(), calls=%async_computation.2 | async-start | bytes 4718592 | tf_op jit(solution)/shard_map/all_gather | solution.py:38
  113.2 52.7 %all-gather.5.cloned.1.call-start = ((), (), s32[]{:S(2)}) async-start(), calls=%async_computation.3 | async-start | bytes 4718592 | tf_op jit(solution)/shard_map/all_gather | solution.py:42
  127.8 13.2 %copy-start.2 = (bf16[384,4096]{1,0:T(8,128)(2,1)S(1)}, bf16[384,4096]{1,0:T(8,128)(2,1)}, u32[]{:S(2)}) copy-start(bf16[384,4096]{1,0:T(8,128)(2,1)} %all-gather.3.cloned.1.call-done) | copy-start | bytes 9437188
  141.0 11.4 %copy-start.1 = (f32[8,2]{0,1:T(2,128)S(1)}, f32[8,2]{0,1:T(2,128)}, u32[]{:S(2)}) copy-start(f32[8,2]{0,1:T(2,128)} %param.11) | copy-start | bytes 196
  152.4 221.7 %reduce-scatter.2.cloned.1.call-start = ((), (), s32[]{:S(2)}) async-start(), calls=%async_computation.4 | async-start | bytes 8912896 | tf_op jit(solution)/shard_map/reduce_scatter | solution.py:49
Sparse Core Ops, SparseCore 0:
  113.3 14.4 all-gather.2
  152.5 13.2 all-gather.4
  192.1 181.9 reduce-scatter.1
